TPU v7x, 128 devices: a whole 4x4x4 slice. The times are simulated.
128 devices in a mesh: row: 8 (over y, core), col: 16 (over x, z).
Axes of the slice: x: 4, y: 4, z: 4, core: 2. Of those that a mesh axis runs over, the one named last changes fastest.
Arguments:
- user_emb: float32 [8, 16, 2048, 128], P('row', 'col'), may hold values from -2.4 to 2.4
- item_emb: float32 [16, 8, 1024, 128], P('col', 'row'), may hold values from -2.4 to 2.4
- tile_vals: bfloat16 [8, 16, 512, 128, 128], P('row', 'col'), may hold values from 0 to 0.029907227
- tile_rows: int32 [8, 16, 512], P('row', 'col'), may hold values from 0 to 255
- tile_cols: int32 [8, 16, 512], P('row', 'col'), may hold values from 0 to 63
- tile_count: int32 [8, 16], P('row', 'col'), may hold values from 128 to 512, as said below
- pair_users: int32 [65536], P(('row', 'col')), may hold values from 0 to 262143, as said below
- pair_items: int32 [65536], P(('row', 'col')), may hold values from 0 to 131071, as said below
- negatives: int32 [1024], replicated, may hold values from 0 to 131071, as said below
Outputs:
- user_final: float32 [8, 16, 2048, 128], P('row', 'col')
- item_final: float32 [16, 8, 1024, 128], P('col', 'row')
- bpr_terms: float32 [65536, 1024], P(('row', 'col'))
Inputs may be any that keep to these rules, and one draw needn't show every extreme that they name: `pair_users`: taken in aligned blocks of 512 entries, at most 8 entries of one block name users that one device holds in user_emb; in every draw some device's users are named exactly 8 times in every block. `pair_items`: taken in aligned blocks of 512 entries, at most 8 entries of one block name items that one device holds in item_emb; in every draw some device's items are named exactly 8 times in every block. `tile_count`: some block has all 512 slots live. `negatives`: entry j names an item that the device with row index (j // 8) // 16 and col index (j // 8) % 16 holds in item_emb.
All inputs are finite; a program needn't handle non-finite values.
Results may differ from a plain program's by a relative error of at most 0.009.
Values may be sent and summed in bfloat16 or wider, within the bound.
A program may use at most 128 MiB of HBM per device.

v0:
```python
import math
import jax
import jax.numpy as jnp
from jax import lax
from jax.sharding import Mesh
from jax.sharding import PartitionSpec as P

ROW = ("row_0", "row_1")
COL = ("col_0", "col_1")
ROW_COL = ("row_0", "row_1", "col_0", "col_1")


def from_everyone(array, axis):
    copies = jnp.broadcast_to(array, (lax.axis_size(axis), *array.shape))
    return lax.all_to_all(copies, axis, split_axis=0, concat_axis=0, tiled=True)


def in_order(blocks, dim):
    blocks = jnp.moveaxis(blocks, 0, dim)
    shape = blocks.shape
    return blocks.reshape(*shape[:dim], shape[dim] * shape[dim + 1], *shape[dim + 2 :])


def collect(array, axis, dim):
    blocks = from_everyone(array, axis)
    return in_order(blocks, dim)


def in_blocks(array, dim, length):
    shape = array.shape
    blocks = array.reshape(*shape[:dim], length, shape[dim] // length, *shape[dim + 1 :])
    return jnp.moveaxis(blocks, dim, 0)


def sent_and_summed(array, axis, dim):
    blocks = in_blocks(array, dim, lax.axis_size(axis))
    arrived = lax.all_to_all(blocks, axis, split_axis=0, concat_axis=0, tiled=True)
    return arrived.astype(jnp.float32).sum(axis=0)


def gather_in_order(array, axes, sequence):
    blocks = array[None]
    for k in sequence:
        blocks = lax.all_gather(blocks, axes[k], axis=0, tiled=True)
    held = [lax.axis_size(axes[k]) for k in reversed(sequence)]
    blocks = blocks.reshape(*held, *array.shape)
    turned = sorted(range(len(sequence)), key=lambda place: sequence[len(sequence) - 1 - place])
    return blocks.transpose(*turned, *range(len(sequence), blocks.ndim)).reshape(-1, *array.shape)


def whole_of(array, axes, sequence, dim):
    return in_order(gather_in_order(array, axes, sequence), dim)


def tile_products(values_all, row_all, col_all, number, user_tiles, item_tiles):
    total = values_all.shape[0]
    width = math.gcd(total, 64)
    blocks = (number + width - 1) // width

    def advance(block_index, totals):
        user_part, item_part = totals
        offset = block_index * width
        values = lax.dynamic_slice_in_dim(values_all, offset, width, 0)
        row_ids = lax.dynamic_slice_in_dim(row_all, offset, width, 0)
        col_ids = lax.dynamic_slice_in_dim(col_all, offset, width, 0)
        live_mask = (offset + jnp.arange(width, dtype=jnp.int32) < number).astype(jnp.float32)[
            :, None, None
        ]
        to_users = (
            jnp.einsum(
                "tij,tje->tie", values, item_tiles[col_ids], preferred_element_type=jnp.float32
            )
            * live_mask
        )
        to_items = (
            jnp.einsum(
                "tij,tie->tje", values, user_tiles[row_ids], preferred_element_type=jnp.float32
            )
            * live_mask
        )
        return (user_part.at[row_ids].add(to_users), item_part.at[col_ids].add(to_items))

    start = (jnp.zeros(user_tiles.shape, jnp.float32), jnp.zeros(item_tiles.shape, jnp.float32))
    return lax.fori_loop(0, blocks, advance, start)


def place_requests(owner, local, devices, slots_per):
    hits = (owner[:, None] == jnp.arange(devices, dtype=jnp.int32)[None, :]).astype(jnp.int32)
    rank = jnp.sum((jnp.cumsum(hits, axis=0) - 1) * hits, axis=1)
    slot = owner * slots_per + rank
    request = jnp.zeros((devices * slots_per,), jnp.int32).at[slot].set(local)
    return (slot, request.reshape(devices, slots_per))


def on_device(
    user_emb,
    item_emb,
    tile_vals,
    tile_rows,
    tile_cols,
    tile_count,
    pair_users,
    pair_items,
    negatives,
):
    row_count = lax.axis_size(ROW)
    col_count = lax.axis_size(COL)
    user_dev = user_emb.shape[2]
    item_dev = item_emb.shape[2]
    embed = user_emb.shape[3]
    tile_side = tile_vals.shape[-1]
    user_whole = lax.all_gather(user_emb.astype(jnp.bfloat16), COL, axis=1, tiled=True)
    item_whole = collect(item_emb.astype(jnp.bfloat16), ROW, 1)
    user_tiles = user_whole.reshape(-1, tile_side, embed)
    item_tiles = item_whole.reshape(-1, tile_side, embed)
    user_part, item_part = tile_products(
        tile_vals[0, 0], tile_rows[0, 0], tile_cols[0, 0], tile_count[0, 0], user_tiles, item_tiles
    )
    user_prop = lax.psum_scatter(
        user_part.reshape(-1, embed).astype(jnp.bfloat16), COL, scatter_dimension=0, tiled=True
    ).astype(jnp.float32)
    item_prop = sent_and_summed(item_part.reshape(-1, embed).astype(jnp.bfloat16), ROW, 0)
    user_final = (user_emb[0, 0] + user_prop) * 0.5
    item_final = (item_emb[0, 0] + item_prop) * 0.5
    devices = row_count * col_count
    slots_per = 2 * pair_users.shape[0] // devices
    user_owner = pair_users // user_dev
    user_local = pair_users % user_dev
    item_holder = pair_items // item_dev
    item_owner = item_holder % row_count * col_count + item_holder // row_count
    item_local = pair_items % item_dev
    user_slot, user_request = place_requests(user_owner, user_local, devices, slots_per)
    item_slot, item_request = place_requests(item_owner, item_local, devices, slots_per)
    user_wanted = lax.all_to_all(user_request, ROW_COL, split_axis=0, concat_axis=0, tiled=True)
    item_wanted = lax.all_to_all(item_request, ROW_COL, split_axis=0, concat_axis=0, tiled=True)
    user_rows = lax.all_to_all(
        user_final[user_wanted].astype(jnp.bfloat16),
        ROW_COL,
        split_axis=0,
        concat_axis=0,
        tiled=True,
    ).astype(jnp.float32)
    item_rows = lax.all_to_all(
        item_final[item_wanted].astype(jnp.bfloat16),
        ROW_COL,
        split_axis=0,
        concat_axis=0,
        tiled=True,
    ).astype(jnp.float32)
    user_vec = user_rows.reshape(-1, embed)[user_slot]
    item_vec = item_rows.reshape(-1, embed)[item_slot]
    offset = (lax.axis_index(COL) * row_count + lax.axis_index(ROW)) * item_dev
    neg_each = negatives.shape[0] // devices
    device_rank = lax.axis_index(ROW) * col_count + lax.axis_index(COL)
    mine = lax.dynamic_slice_in_dim(negatives, device_rank * neg_each, neg_each, 0) - offset
    negative_vec = whole_of(item_final[mine], ROW_COL, (0, 2, 3, 1), 0)
    positive = jnp.sum(user_vec * item_vec, axis=1)
    against = jnp.dot(user_vec, negative_vec.T, precision=lax.Precision.HIGHEST)
    bpr_terms = jnp.log1p(jnp.exp(against - positive[:, None]))
    return (user_final.reshape(user_emb.shape), item_final.reshape(item_emb.shape), bpr_terms)


def solution(mesh):
    torus = Mesh(mesh.devices.reshape(4, 2, 4, 4), ("row_0", "row_1", "col_0", "col_1"))
    return jax.shard_map(
        on_device,
        mesh=torus,
        in_specs=(
            P(ROW, COL, None, None),
            P(COL, ROW, None, None),
            P(ROW, COL, None, None, None),
            P(ROW, COL, None),
            P(ROW, COL, None),
            P(ROW, COL),
            P(ROW_COL),
            P(ROW_COL),
            P(),
        ),
        out_specs=(P(ROW, COL, None, None), P(COL, ROW, None, None), P(ROW_COL, None)),
        check_vma=False,
    )
```

profile of v0, /device:TPU:1, one launch (start us, length us, event | category | flops | bytes accessed | tf_op | source)
XLA Modules:
  0.0 615.4 jit_solution(11518100190499439016)
XLA Ops:
  7.2 2.1 bitcast_convert_fusion
  9.3 1.1 convert_bitcast_fusion.2
  10.4 1.6 broadcast_in_dim.25
  12.0 6.0 all-to-all-start
  18.6 25.5 %all-to-all-done = bf16[8,1,1,1024,128]{4,3,2,1,0:T(8,128)(2,1)S(1)} async-done(((bf16[8,1,1,1024,128]{4,3,2,1,0:T(8,128)(2,1)}), bf16[8,1,1,1024,128]{4,3,2,1,0:T(8,128)(2,1)S(1)}, u32[]{:S(2)}, u32[]{:S(2)}) %all-to-all-start) | async-done | bytes 2097184 | tf_op jit(solution)/shard_map/all_to_all | solution.py:15
  44.1 40.6 %all-gather.3.cloned.1.call-done = bf16[1,16,2048,128]{3,2,0,1:T(8,128)(2,1)} async-done(((bf16[1,1,2048,128]{3,2,0,1:T(8,128)(2,1)}), bf16[1,16,2048,128]{3,2,0,1:T(8,128)(2,1)}) %all-gather.3.cloned.1.call-update) | async-done | bytes 8388624 | tf_op jit(solution)/shard_map/all_gather | solution.py:112
  84.7 7.8 %broadcast_in_dim.23 = f32[256,128,128]{2,1,0:T(8,128)} broadcast(f32[]{:T(128)} %constant.123.clone.1), dimensions={} | broadcast | bytes 16777220 | tf_op jit(solution)/shard_map/broadcast_in_dim | solution.py:83
  92.5 2.5 broadcast_in_dim.24
  95.0 135.0 %while.12 = (s32[]{:T(128)}, f32[256,128,128]{2,1,0:T(8,128)}, f32[64,128,128]{2,1,0:T(8,128)}, s32[]{:T(128)}, s32[512]{0:T(512)}, /*index=5*/bf16[512,128,128]...) while((s32[]{:T(128)}, f32[256,128,128]{2,1,0:T(8,128)}, ...), condition=%wide.region_3.4_spmd, body=%wide.region_0.3_spmd.sunk | while | flops 541067840 | bytes 67120640 | solution.py:84
  95.0 0.8 compare_select_fusion.8
  96.3 2.5 gather_fusion
  98.9 0.7 compare_convert_fusion.2
  99.5 4.2 convolution_multiply_fusion.4
  103.8 13.7 %scatter_fusion = f32[256,128,128]{2,1,0:T(8,128)} fusion(f32[256,128,128]{2,1,0:T(8,128)} %get-tuple-element.166, s32[64]{0:T(128)S(1)} %get-tuple-element.149, f32[64,128,128]{2,1,0:T(8,128)} %convolution_multiply_fusion.4), kind=kCustom, calls=%fused_computation.8.clone.1 | custom fusion | flops 1048576 | bytes 12583168 | tf_op jit(solution)/shard_map/while/body/scatter-add | solution.py:81
  117.5 4.3 gather_fusion.1
  121.9 4.6 convolution_multiply_fusion.5
  126.5 13.6 %scatter_fusion.1 = f32[64,128,128]{2,1,0:T(8,128)} fusion(f32[64,128,128]{2,1,0:T(8,128)} %get-tuple-element.167, s32[64]{0:T(128)S(1)} %get-tuple-element.150, f32[64,128,128]{2,1,0:T(8,128)} %convolution_multiply_fusion.5), kind=kCustom, calls=%fused_computation.9.clone.1 | custom fusion | flops 1048576 | bytes 12583168 | tf_op jit(solution)/shard_map/while/body/scatter-add | solution.py:81
  140.0 0.8 compare_select_fusion.8
  140.9 0.5 copy-done
  141.4 2.5 gather_fusion
  143.9 0.7 compare_convert_fusion.2
  144.6 4.2 convolution_multiply_fusion.4
  148.8 13.6 %scatter_fusion = f32[256,128,128]{2,1,0:T(8,128)} fusion(f32[256,128,128]{2,1,0:T(8,128)} %get-tuple-element.166, s32[64]{0:T(128)S(1)} %get-tuple-element.149, f32[64,128,128]{2,1,0:T(8,128)} %convolution_multiply_fusion.4), kind=kCustom, calls=%fused_computation.8.clone.1 | custom fusion | flops 1048576 | bytes 12583168 | tf_op jit(solution)/shard_map/while/body/scatter-add | solution.py:81
  162.5 4.3 gather_fusion.1
  166.8 4.6 convolution_multiply_fusion.5
  171.4 13.6 %scatter_fusion.1 = f32[64,128,128]{2,1,0:T(8,128)} fusion(f32[64,128,128]{2,1,0:T(8,128)} %get-tuple-element.167, s32[64]{0:T(128)S(1)} %get-tuple-element.150, f32[64,128,128]{2,1,0:T(8,128)} %convolution_multiply_fusion.5), kind=kCustom, calls=%fused_computation.9.clone.1 | custom fusion | flops 1048576 | bytes 12583168 | tf_op jit(solution)/shard_map/while/body/scatter-add | solution.py:81
  185.0 0.8 compare_select_fusion.8
  186.3 2.5 gather_fusion
  188.9 0.7 compare_convert_fusion.2
  189.5 4.2 convolution_multiply_fusion.4
  193.8 13.6 %scatter_fusion = f32[256,128,128]{2,1,0:T(8,128)} fusion(f32[256,128,128]{2,1,0:T(8,128)} %get-tuple-element.166, s32[64]{0:T(128)S(1)} %get-tuple-element.149, f32[64,128,128]{2,1,0:T(8,128)} %convolution_multiply_fusion.4), kind=kCustom, calls=%fused_computation.8.clone.1 | custom fusion | flops 1048576 | bytes 12583168 | tf_op jit(solution)/shard_map/while/body/scatter-add | solution.py:81
  207.4 4.3 gather_fusion.1
  211.7 4.6 convolution_multiply_fusion.5
  216.3 13.7 %scatter_fusion.1 = f32[64,128,128]{2,1,0:T(8,128)} fusion(f32[64,128,128]{2,1,0:T(8,128)} %get-tuple-element.167, s32[64]{0:T(128)S(1)} %get-tuple-element.150, f32[64,128,128]{2,1,0:T(8,128)} %convolution_multiply_fusion.5), kind=kCustom, calls=%fused_computation.9.clone.1 | custom fusion | flops 1048576 | bytes 12583168 | tf_op jit(solution)/shard_map/while/body/scatter-add | solution.py:81
  230.0 9.2 %convert_element_type.55 = bf16[256,128,128]{2,1,0:T(8,128)(2,1)} convert(f32[256,128,128]{2,1,0:T(8,128)} %get-tuple-element.57) | non-fusion elementwise | flops 4194304 | bytes 25165824 | tf_op jit(solution)/shard_map/convert_element_type | solution.py:120
  239.2 0.7 copy-done.4
  240.6 2.4 scatter_custom_fusion.2
  243.0 0.7 all_to_all.30
  243.7 232.4 %all-to-all-start.2 = ((s32[128,1,8]{2,1,0:T(1,128)}), s32[128,1,8]{2,1,0:T(1,128)S(1)}, u32[]{:S(2)}, u32[]{:S(2)}) async-start(s32[128,1,8]{2,1,0:T(1,128)} %bitcast.17), calls=%async_computation.3 | async-start | bytes 131072 | tf_op jit(solution)/shard_map/all_to_all | solution.py:134
  476.9 2.4 scatter_custom_fusion.3
  479.3 0.7 all_to_all.34
  480.0 5.6 all-to-all-done.2
  485.6 4.6 all-to-all-start.4
  490.3 4.0 convert_element_type.58
  494.2 5.7 all-to-all-done.4
  499.9 4.7 all-to-all-start.1
  504.6 0.8 compare_select_fusion.6
  505.6 25.2 %all-to-all-done.1 = bf16[8,1024,128]{2,1,0:T(8,128)(2,1)S(1)} async-done(((bf16[8,1024,128]{2,1,0:T(8,128)(2,1)}), bf16[8,1024,128]{2,1,0:T(8,128)(2,1)S(1)}, u32[]{:S(2)}, u32[]{:S(2)}) %all-to-all-start.1) | async-done | bytes 2097184 | tf_op jit(solution)/shard_map/all_to_all | solution.py:37
  531.2 4.0 gather_fusion.6
  535.2 4.4 all-to-all-start.5
  539.6 0.6 gather_fusion.4
  540.2 10.7 %all-gather = f32[32,128]{1,0:T(8,128)S(1)} all-gather(f32[8,128]{1,0:T(8,128)S(1)} %gather_fusion.4), channel_id=2, replica_groups=mesh['row_0'=4,'row_1'=2,'col_0'=4,'col_1'=4] {'row_0'}, dimensions={0}, use_global_device_ids=true | all-gather | bytes 20480 | tf_op jit(solution)/shard_map/all_gather | solution.py:44
  550.8 9.0 %all_gather.17 = f32[16,8,128]{2,1,0:T(8,128)S(1)} all-gather(f32[4,8,128]{2,1,0:T(8,128)S(1)} %bitcast.86), channel_id=1, replica_groups=mesh['row_0'=4,'row_1'=2,'col_0'=4,'col_1'=4] {'col_0'}, dimensions={0}, use_global_device_ids=true | all-gather | bytes 81920 | tf_op jit(solution)/shard_map/all_gather | solution.py:44
  559.8 10.2 %all_gather.18 = f32[64,8,128]{2,1,0:T(8,128)S(1)} all-gather(f32[16,8,128]{2,1,0:T(8,128)S(1)} %all_gather.17), channel_id=1, replica_groups=mesh['row_0'=4,'row_1'=2,'col_0'=4,'col_1'=4] {'col_1'}, dimensions={0}, use_global_device_ids=true | all-gather | bytes 327680 | tf_op jit(solution)/shard_map/all_gather | solution.py:44
  570.0 0.8 fusion.6
  570.9 1.5 fusion.4
  572.3 4.1 gather_fusion.2
  576.4 15.6 %all-to-all-start.3 = ((bf16[128,8,128]{2,1,0:T(8,128)(2,1)}), bf16[128,8,128]{2,1,0:T(8,128)(2,1)S(1)}, u32[]{:S(2)}, u32[]{:S(2)}) async-start(bf16[128,8,128]{2,1,0:T(8,128)(2,1)} %bitcast.66), calls=%async_computation.4 | async-start | bytes 524288 | tf_op jit(solution)/shard_map/all_to_all | solution.py:136
  592.1 2.9 all_gather.19
  595.0 1.0 gather_fusion.7
  596.1 6.8 %all-to-all-done.3 = bf16[128,8,128]{2,1,0:T(8,128)(2,1)S(1)} async-done(((bf16[128,8,128]{2,1,0:T(8,128)(2,1)}), bf16[128,8,128]{2,1,0:T(8,128)(2,1)S(1)}, u32[]{:S(2)}, u32[]{:S(2)}) %all-to-all-start.3) | async-done | bytes 262176 | tf_op jit(solution)/shard_map/all_to_all | solution.py:136
  603.0 1.0 gather_fusion.5
  604.0 1.3 gather_fusion.3
  605.5 3.1 exponential_log-plus-one_fusion
  (65 shorter events, 3.4 us)
Async XLA Ops:
  7.2 77.5 %all-gather.3.cloned.1.call-start = ((), (), s32[]{:S(2)}) async-start(), calls=%async_computation.7 | async-start | bytes 8912896 | tf_op jit(solution)/shard_map/all_gather | solution.py:112
  12.0 32.2 %all-to-all-start = ((bf16[8,1,1,1024,128]{4,3,2,1,0:T(8,128)(2,1)}), bf16[8,1,1,1024,128]{4,3,2,1,0:T(8,128)(2,1)S(1)}, u32[]{:S(2)}, u32[]{:S(2)}) async-start(bf16[8,1,1,1024,128]{4,3,2,1,0:T(8,128)(2,1)} %broadcast_in_dim.25), calls=%async_computation | async-start | bytes 4194304 | tf_op jit(solution)/shard_map/all_to_all | solution.py:15
  17.9 552.9 %reduce-scatter.2.cloned.1.call-start = ((), (), s32[]{:S(2)}) async-start(), calls=%async_computation.8 | async-start | bytes 8912896 | tf_op jit(solution)/shard_map/reduce_scatter | solution.py:119
  95.0 1.3 copy-start
  126.5 13.6 %copy-start.1 = (bf16[64,128,128]{2,1,0:T(8,128)(2,1)S(1)}, bf16[64,128,128]{2,1,0:T(8,128)(2,1)}, u32[]{:S(2)}) copy-start(bf16[64,128,128]{2,1,0:T(8,128)(2,1)} %copy-done) | copy-start | bytes 6291460 | tf_op jit(solution)/shard_map/while
  140.0 1.3 copy-start
  171.4 13.6 %copy-start.1 = (bf16[64,128,128]{2,1,0:T(8,128)(2,1)S(1)}, bf16[64,128,128]{2,1,0:T(8,128)(2,1)}, u32[]{:S(2)}) copy-start(bf16[64,128,128]{2,1,0:T(8,128)(2,1)} %copy-done) | copy-start | bytes 6291460 | tf_op jit(solution)/shard_map/while
  185.0 1.3 copy-start
  216.3 13.7 %copy-start.1 = (bf16[64,128,128]{2,1,0:T(8,128)(2,1)S(1)}, bf16[64,128,128]{2,1,0:T(8,128)(2,1)}, u32[]{:S(2)}) copy-start(bf16[64,128,128]{2,1,0:T(8,128)(2,1)} %copy-done) | copy-start | bytes 6291460 | tf_op jit(solution)/shard_map/while
  239.2 0.7 copy-start.4
  239.2 236.9 %copy-start.5 = (s32[512]{0:T(512)S(1)}, s32[512]{0:T(512)}, u32[]{:S(2)}) copy-start(s32[512]{0:T(512)} %param.18) | copy-start | bytes 6148
  243.7 241.9 %all-to-all-start.2 = ((s32[128,1,8]{2,1,0:T(1,128)}), s32[128,1,8]{2,1,0:T(1,128)S(1)}, u32[]{:S(2)}, u32[]{:S(2)}) async-start(s32[128,1,8]{2,1,0:T(1,128)} %bitcast.17), calls=%async_computation.3 | async-start | bytes 131072 | tf_op jit(solution)/shard_map/all_to_all | solution.py:134
  485.6 14.3 %all-to-all-start.4 = ((s32[128,1,8]{2,1,0:T(1,128)}), s32[128,1,8]{2,1,0:T(1,128)S(1)}, u32[]{:S(2)}, u32[]{:S(2)}) async-start(s32[128,1,8]{2,1,0:T(1,128)} %bitcast.30), calls=%async_computation.5 | async-start | bytes 131072 | tf_op jit(solution)/shard_map/all_to_all | solution.py:135
  494.2 36.9 %copy-start.3 = (f32[1,1,1024,128]{3,2,1,0:T(8,128)S(1)}, f32[1,1,1024,128]{3,2,1,0:T(8,128)}, u32[]{:S(2)}) copy-start(f32[1,1,1024,128]{3,2,1,0:T(8,128)} %param.12) | copy-start | bytes 1572868
  499.9 30.9 %all-to-all-start.1 = ((bf16[8,1024,128]{2,1,0:T(8,128)(2,1)}), bf16[8,1024,128]{2,1,0:T(8,128)(2,1)S(1)}, u32[]{:S(2)}, u32[]{:S(2)}) async-start(bf16[8,1024,128]{2,1,0:T(8,128)(2,1)} %bitcast.11), calls=%async_computation.2 | async-start | bytes 4194304 | tf_op jit(solution)/shard_map/all_to_all | solution.py:37
  535.2 41.2 %all-to-all-start.5 = ((bf16[128,8,128]{2,1,0:T(8,128)(2,1)}), bf16[128,8,128]{2,1,0:T(8,128)(2,1)S(1)}, u32[]{:S(2)}, u32[]{:S(2)}) async-start(bf16[128,8,128]{2,1,0:T(8,128)(2,1)} %bitcast.65), calls=%async_computation.6 | async-start | bytes 524288 | tf_op jit(solution)/shard_map/all_to_all | solution.py:143
  572.3 30.6 %copy-start.2 = (f32[2048,128]{1,0:T(8,128)}, f32[2048,128]{1,0:T(8,128)S(1)}, u32[]{:S(2)}) copy-start(f32[2048,128]{1,0:T(8,128)S(1)} %fusion.4) | copy-start | bytes 3145732
  576.4 26.5 %all-to-all-start.3 = ((bf16[128,8,128]{2,1,0:T(8,128)(2,1)}), bf16[128,8,128]{2,1,0:T(8,128)(2,1)S(1)}, u32[]{:S(2)}, u32[]{:S(2)}) async-start(bf16[128,8,128]{2,1,0:T(8,128)(2,1)} %bitcast.66), calls=%async_computation.4 | async-start | bytes 524288 | tf_op jit(solution)/shard_map/all_to_all | solution.py:136
Sparse Core Ops, SparseCore 0:
  10.7 73.9 all-gather.2
  239.3 311.7 reduce-scatter.1
where the time goes:
time: 619 us; the launch traced here: 615 us
  starting transfers between devices  268 us (43%)
  waiting for transfers between devices  109 us (18%)
  other arithmetic  107 us (17%)
  local copies, waits for them, and re-layouts  53.6 us (9%)
  blocking collectives  32.7 us (5%)
  matrix products  29.6 us (5%)
  between operations  15 us (2%)
    all_to_all x1, starting transfers between devices, on_device(): lax.all_to_all(user_request, ROW_COL, split_axis=0, concat_axis=0, tiled=...  232 us
    scatter-add x3, other arithmetic, advance(): user_part.at[row_ids].add(to_users)  41 us
    scatter-add x3, other arithmetic, advance(): item_part.at[col_ids].add(to_items)  40.8 us
    all_gather x1, waiting for transfers between devices, on_device(): lax.all_gather(user_emb.astype(jnp.bfloat16), COL, axis=1, tiled=True)  40.6 us
    all_gather x4, blocking collectives, gather_in_order(): blocks = lax.all_gather(blocks, axes[k], axis=0, tiled=True)  32.7 us
    all_to_all x1, waiting for transfers between devices, from_everyone(): return lax.all_to_all(copies, axis, split_axis=0, concat_axis=0, tiled=True)  25.5 us
    all_to_all x1, waiting for transfers between devices, sent_and_summed(): lax.all_to_all(blocks, axis, split_axis=0, concat_axis=0, tiled=True)  25.2 us
    all_to_all x1, starting transfers between devices, on_device(): lax.all_to_all(user_final[user_wanted].astype(jnp.bfloat16), ROW_COL, spl...  15.6 us
  transfers between devices with their start and end apart: 8, of which 6 were waited for; matrix products, arithmetic and copies ran while one was open for 4% of the time, Pallas kernels for 0%

commit v1 on v0

--- a/solution.py
+++ b/solution.py
@@ -109,7 +109,10 @@
     item_dev = item_emb.shape[2]
     embed = user_emb.shape[3]
     tile_side = tile_vals.shape[-1]
-    user_whole = lax.all_gather(user_emb.astype(jnp.bfloat16), COL, axis=1, tiled=True)
+    user_whole = jnp.concatenate(
+        lax.all_to_all(jnp.stack([user_emb.astype(jnp.bfloat16)] * lax.axis_size(COL)), COL, 0, 0),
+        axis=1,
+    )
     item_whole = collect(item_emb.astype(jnp.bfloat16), ROW, 1)
     user_tiles = user_whole.reshape(-1, tile_side, embed)
     item_tiles = item_whole.reshape(-1, tile_side, embed)

time: 619 us -> 738 us (1.19)
  waiting for transfers between devices: 109 us -> 210 us
  starting transfers between devices: 268 us -> 280 us
    all_to_all x0 -> x1, waiting for transfers between devices: none -> 142 us  [on_device(): lax.all_to_all(jnp.stack([user_emb.astype(jnp.bfloat16)] * lax.axis_size(...]
    all_gather x1 -> x0, waiting for transfers between devices: 40.6 us -> none  [on_device(): lax.all_gather(user_emb.astype(jnp.bfloat16), COL, axis=1, tiled=True)]
    all_to_all x0 -> x1, starting transfers between devices: none -> 7.65 us  [on_device(): lax.all_to_all(jnp.stack([user_emb.astype(jnp.bfloat16)] * lax.axis_size(...]
  transfers between devices with their start and end apart: 8 -> 8, of which waited for: 6 -> 6; matrix products, arithmetic and copies ran while one was open for 4% -> 3% of each run, Pallas kernels for 0% -> 0%
where the time goes in v1:
time: 738 us; the launch traced here: 734 us
  starting transfers between devices  280 us (38%)
  waiting for transfers between devices  210 us (28%)
  other arithmetic  106 us (14%)
  local copies, waits for them, and re-layouts  59.5 us (8%)
  blocking collectives  32.7 us (4%)
  matrix products  29.6 us (4%)
  between operations  15 us (2%)
    all_to_all x1, starting transfers between devices, on_device(): lax.all_to_all(user_request, ROW_COL, split_axis=0, concat_axis=0, tiled=...  238 us
    all_to_all x1, waiting for transfers between devices, on_device(): lax.all_to_all(jnp.stack([user_emb.astype(jnp.bfloat16)] * lax.axis_size(...  142 us
    scatter-add x3, other arithmetic, advance(): user_part.at[row_ids].add(to_users)  41 us
    scatter-add x3, other arithmetic, advance(): item_part.at[col_ids].add(to_items)  40.8 us
    all_gather x4, blocking collectives, gather_in_order(): blocks = lax.all_gather(blocks, axes[k], axis=0, tiled=True)  32.7 us
    all_to_all x1, waiting for transfers between devices, from_everyone(): return lax.all_to_all(copies, axis, split_axis=0, concat_axis=0, tiled=True)  25.4 us
    all_to_all x1, waiting for transfers between devices, sent_and_summed(): lax.all_to_all(blocks, axis, split_axis=0, concat_axis=0, tiled=True)  25.2 us
    all_to_all x1, starting transfers between devices, on_device(): lax.all_to_all(user_final[user_wanted].astype(jnp.bfloat16), ROW_COL, spl...  15.7 us
  transfers between devices with their start and end apart: 8, of which 6 were waited for; matrix products, arithmetic and copies ran while one was open for 3% of the time, Pallas kernels for 0%

profile of v1, /device:TPU:1, one launch (start us, length us, event | category | flops | bytes accessed | tf_op | source)
XLA Modules:
  0.0 733.8 jit_solution(10728154804819847810)
XLA Ops:
  7.2 1.2 convert_bitcast_fusion.3
  8.3 1.6 broadcast_in_dim.25
  9.9 6.0 all-to-all-start
  15.9 0.8 convert_bitcast_fusion
  16.7 25.4 %all-to-all-done = bf16[8,1,1,1024,128]{4,3,2,1,0:T(8,128)(2,1)S(1)} async-done(((bf16[8,1,1,1024,128]{4,3,2,1,0:T(8,128)(2,1)}), bf16[8,1,1,1024,128]{4,3,2,1,0:T(8,128)(2,1)S(1)}, u32[]{:S(2)}, u32[]{:S(2)}) %all-to-all-start) | async-done | bytes 2097184 | tf_op jit(solution)/shard_map/all_to_all | solution.py:15
  42.1 5.9 stack.2
  48.0 7.6 %all-to-all-start.1 = ((bf16[16,1,1,2048,128]{4,3,2,1,0:T(8,128)(2,1)}), bf16[16,1,1,2048,128]{4,3,2,1,0:T(8,128)(2,1)}, u32[]{:S(2)}, u32[]{:S(2)}) async-start(bf16[16,1,1,2048,128]{4,3,2,1,0:T(8,128)(2,1)} %stack.2), calls=%async_computation.1 | async-start | bytes 16777216 | tf_op jit(solution)/shard_map/all_to_all | solution.py:113
  56.3 141.6 %all-to-all-done.1 = bf16[16,1,1,2048,128]{4,3,2,1,0:T(8,128)(2,1)} async-done(((bf16[16,1,1,2048,128]{4,3,2,1,0:T(8,128)(2,1)}), bf16[16,1,1,2048,128]{4,3,2,1,0:T(8,128)(2,1)}, u32[]{:S(2)}, u32[]{:S(2)}) %all-to-all-start.1) | async-done | bytes 8388640 | tf_op jit(solution)/shard_map/all_to_all | solution.py:113
  197.9 7.8 %broadcast_in_dim.23 = f32[256,128,128]{2,1,0:T(8,128)} broadcast(f32[]{:T(128)} %constant.123.clone.1), dimensions={} | broadcast | bytes 16777220 | tf_op jit(solution)/shard_map/broadcast_in_dim | solution.py:83
  205.8 2.5 broadcast_in_dim.24
  208.3 135.0 %while.12 = (s32[]{:T(128)}, f32[256,128,128]{2,1,0:T(8,128)}, f32[64,128,128]{2,1,0:T(8,128)}, s32[]{:T(128)}, s32[512]{0:T(512)}, /*index=5*/bf16[512,128,128]...) while((s32[]{:T(128)}, f32[256,128,128]{2,1,0:T(8,128)}, ...), condition=%wide.region_3.4_spmd, body=%wide.region_0.3_spmd.sunk | while | flops 541067840 | bytes 67120640 | solution.py:84
  208.3 0.8 compare_select_fusion.8
  209.6 2.5 gather_fusion
  212.1 0.7 compare_convert_fusion.2
  212.8 4.2 convolution_multiply_fusion.4
  217.0 13.7 %scatter_fusion = f32[256,128,128]{2,1,0:T(8,128)} fusion(f32[256,128,128]{2,1,0:T(8,128)} %get-tuple-element.166, s32[64]{0:T(128)S(1)} %get-tuple-element.149, f32[64,128,128]{2,1,0:T(8,128)} %convolution_multiply_fusion.4), kind=kCustom, calls=%fused_computation.8.clone.1 | custom fusion | flops 1048576 | bytes 12583168 | tf_op jit(solution)/shard_map/while/body/scatter-add | solution.py:81
  230.8 4.3 gather_fusion.1
  235.1 4.6 convolution_multiply_fusion.5
  239.7 13.6 %scatter_fusion.1 = f32[64,128,128]{2,1,0:T(8,128)} fusion(f32[64,128,128]{2,1,0:T(8,128)} %get-tuple-element.167, s32[64]{0:T(128)S(1)} %get-tuple-element.150, f32[64,128,128]{2,1,0:T(8,128)} %convolution_multiply_fusion.5), kind=kCustom, calls=%fused_computation.9.clone.1 | custom fusion | flops 1048576 | bytes 12583168 | tf_op jit(solution)/shard_map/while/body/scatter-add | solution.py:81
  253.3 0.8 compare_select_fusion.8
  254.6 2.5 gather_fusion
  257.1 0.7 compare_convert_fusion.2
  257.8 4.2 convolution_multiply_fusion.4
  262.0 13.6 %scatter_fusion = f32[256,128,128]{2,1,0:T(8,128)} fusion(f32[256,128,128]{2,1,0:T(8,128)} %get-tuple-element.166, s32[64]{0:T(128)S(1)} %get-tuple-element.149, f32[64,128,128]{2,1,0:T(8,128)} %convolution_multiply_fusion.4), kind=kCustom, calls=%fused_computation.8.clone.1 | custom fusion | flops 1048576 | bytes 12583168 | tf_op jit(solution)/shard_map/while/body/scatter-add | solution.py:81
  275.7 4.3 gather_fusion.1
  280.0 4.6 convolution_multiply_fusion.5
  284.6 13.6 %scatter_fusion.1 = f32[64,128,128]{2,1,0:T(8,128)} fusion(f32[64,128,128]{2,1,0:T(8,128)} %get-tuple-element.167, s32[64]{0:T(128)S(1)} %get-tuple-element.150, f32[64,128,128]{2,1,0:T(8,128)} %convolution_multiply_fusion.5), kind=kCustom, calls=%fused_computation.9.clone.1 | custom fusion | flops 1048576 | bytes 12583168 | tf_op jit(solution)/shard_map/while/body/scatter-add | solution.py:81
  298.2 0.8 compare_select_fusion.8
  299.6 2.5 gather_fusion
  302.1 0.7 compare_convert_fusion.2
  302.8 4.2 convolution_multiply_fusion.4
  307.0 13.6 %scatter_fusion = f32[256,128,128]{2,1,0:T(8,128)} fusion(f32[256,128,128]{2,1,0:T(8,128)} %get-tuple-element.166, s32[64]{0:T(128)S(1)} %get-tuple-element.149, f32[64,128,128]{2,1,0:T(8,128)} %convolution_multiply_fusion.4), kind=kCustom, calls=%fused_computation.8.clone.1 | custom fusion | flops 1048576 | bytes 12583168 | tf_op jit(solution)/shard_map/while/body/scatter-add | solution.py:81
  320.6 4.3 gather_fusion.1
  325.0 4.6 convolution_multiply_fusion.5
  329.6 13.7 %scatter_fusion.1 = f32[64,128,128]{2,1,0:T(8,128)} fusion(f32[64,128,128]{2,1,0:T(8,128)} %get-tuple-element.167, s32[64]{0:T(128)S(1)} %get-tuple-element.150, f32[64,128,128]{2,1,0:T(8,128)} %convolution_multiply_fusion.5), kind=kCustom, calls=%fused_computation.9.clone.1 | custom fusion | flops 1048576 | bytes 12583168 | tf_op jit(solution)/shard_map/while/body/scatter-add | solution.py:81
  343.2 9.2 %convert_element_type.58 = bf16[256,128,128]{2,1,0:T(8,128)(2,1)} convert(f32[256,128,128]{2,1,0:T(8,128)} %get-tuple-element.57) | non-fusion elementwise | flops 4194304 | bytes 25165824 | tf_op jit(solution)/shard_map/convert_element_type | solution.py:123
  352.4 0.7 copy-done.5
  353.8 2.4 scatter_custom_fusion.2
  356.3 0.7 all_to_all.34
  357.0 237.5 %all-to-all-start.3 = ((s32[128,1,8]{2,1,0:T(1,128)}), s32[128,1,8]{2,1,0:T(1,128)S(1)}, u32[]{:S(2)}, u32[]{:S(2)}) async-start(s32[128,1,8]{2,1,0:T(1,128)} %bitcast.17), calls=%async_computation.4 | async-start | bytes 131072 | tf_op jit(solution)/shard_map/all_to_all | solution.py:137
  595.3 2.4 scatter_custom_fusion.3
  597.7 0.7 all_to_all.38
  598.4 5.6 all-to-all-done.3
  604.0 4.6 all-to-all-start.5
  608.6 4.0 convert_element_type.61
  612.6 5.7 all-to-all-done.5
  618.3 4.7 all-to-all-start.2
  623.0 0.8 compare_select_fusion.6
  624.0 25.2 %all-to-all-done.2 = bf16[8,1024,128]{2,1,0:T(8,128)(2,1)S(1)} async-done(((bf16[8,1024,128]{2,1,0:T(8,128)(2,1)}), bf16[8,1024,128]{2,1,0:T(8,128)(2,1)S(1)}, u32[]{:S(2)}, u32[]{:S(2)}) %all-to-all-start.2) | async-done | bytes 2097184 | tf_op jit(solution)/shard_map/all_to_all | solution.py:37
  649.6 4.0 gather_fusion.6
  653.6 4.4 all-to-all-start.6
  658.6 10.7 %all-gather = f32[32,128]{1,0:T(8,128)S(1)} all-gather(f32[8,128]{1,0:T(8,128)S(1)} %gather_fusion.4), channel_id=2, replica_groups=mesh['row_0'=4,'row_1'=2,'col_0'=4,'col_1'=4] {'row_0'}, dimensions={0}, use_global_device_ids=true | all-gather | bytes 20480 | tf_op jit(solution)/shard_map/all_gather | solution.py:44
  669.2 9.1 %all_gather.13 = f32[16,8,128]{2,1,0:T(8,128)S(1)} all-gather(f32[4,8,128]{2,1,0:T(8,128)S(1)} %bitcast.85), channel_id=1, replica_groups=mesh['row_0'=4,'row_1'=2,'col_0'=4,'col_1'=4] {'col_0'}, dimensions={0}, use_global_device_ids=true | all-gather | bytes 81920 | tf_op jit(solution)/shard_map/all_gather | solution.py:44
  678.3 10.1 %all_gather.14 = f32[64,8,128]{2,1,0:T(8,128)S(1)} all-gather(f32[16,8,128]{2,1,0:T(8,128)S(1)} %all_gather.13), channel_id=1, replica_groups=mesh['row_0'=4,'row_1'=2,'col_0'=4,'col_1'=4] {'col_1'}, dimensions={0}, use_global_device_ids=true | all-gather | bytes 327680 | tf_op jit(solution)/shard_map/all_gather | solution.py:44
  688.4 0.8 fusion.6
  689.3 1.5 fusion.4
  690.7 4.1 gather_fusion.2
  694.8 15.7 %all-to-all-start.4 = ((bf16[128,8,128]{2,1,0:T(8,128)(2,1)}), bf16[128,8,128]{2,1,0:T(8,128)(2,1)S(1)}, u32[]{:S(2)}, u32[]{:S(2)}) async-start(bf16[128,8,128]{2,1,0:T(8,128)(2,1)} %bitcast.66), calls=%async_computation.5 | async-start | bytes 524288 | tf_op jit(solution)/shard_map/all_to_all | solution.py:139
  710.5 2.9 all_gather.15
  713.5 1.0 gather_fusion.7
  714.5 6.8 all-to-all-done.4
  721.4 1.0 gather_fusion.5
  722.4 1.3 gather_fusion.3
  723.9 3.1 exponential_log-plus-one_fusion
  (67 shorter events, 4.4 us)
Async XLA Ops:
  7.2 8.7 %copy-start.4 = (f32[1,1,2048,128]{3,2,1,0:T(8,128)S(1)}, f32[1,1,2048,128]{3,2,1,0:T(8,128)}, u32[]{:S(2)}) copy-start(f32[1,1,2048,128]{3,2,1,0:T(8,128)} %param.11) | copy-start | bytes 3145732
  9.9 32.2 %all-to-all-start = ((bf16[8,1,1,1024,128]{4,3,2,1,0:T(8,128)(2,1)}), bf16[8,1,1,1024,128]{4,3,2,1,0:T(8,128)(2,1)S(1)}, u32[]{:S(2)}, u32[]{:S(2)}) async-start(bf16[8,1,1,1024,128]{4,3,2,1,0:T(8,128)(2,1)} %broadcast_in_dim.25), calls=%async_computation | async-start | bytes 4194304 | tf_op jit(solution)/shard_map/all_to_all | solution.py:15
  48.0 149.9 %all-to-all-start.1 = ((bf16[16,1,1,2048,128]{4,3,2,1,0:T(8,128)(2,1)}), bf16[16,1,1,2048,128]{4,3,2,1,0:T(8,128)(2,1)}, u32[]{:S(2)}, u32[]{:S(2)}) async-start(bf16[16,1,1,2048,128]{4,3,2,1,0:T(8,128)(2,1)} %stack.2), calls=%async_computation.1 | async-start | bytes 16777216 | tf_op jit(solution)/shard_map/all_to_all | solution.py:113
  55.6 633.6 %reduce-scatter.2.cloned.1.call-start = ((), (), s32[]{:S(2)}) async-start(), calls=%async_computation.8 | async-start | bytes 8912896 | tf_op jit(solution)/shard_map/reduce_scatter | solution.py:122
  208.3 1.3 copy-start
  239.7 13.6 %copy-start.1 = (bf16[64,128,128]{2,1,0:T(8,128)(2,1)S(1)}, bf16[64,128,128]{2,1,0:T(8,128)(2,1)}, u32[]{:S(2)}) copy-start(bf16[64,128,128]{2,1,0:T(8,128)(2,1)} %copy-done) | copy-start | bytes 6291460 | tf_op jit(solution)/shard_map/while
  253.3 1.3 copy-start
  284.6 13.6 %copy-start.1 = (bf16[64,128,128]{2,1,0:T(8,128)(2,1)S(1)}, bf16[64,128,128]{2,1,0:T(8,128)(2,1)}, u32[]{:S(2)}) copy-start(bf16[64,128,128]{2,1,0:T(8,128)(2,1)} %copy-done) | copy-start | bytes 6291460 | tf_op jit(solution)/shard_map/while
  298.2 1.3 copy-start
  329.6 13.7 %copy-start.1 = (bf16[64,128,128]{2,1,0:T(8,128)(2,1)S(1)}, bf16[64,128,128]{2,1,0:T(8,128)(2,1)}, u32[]{:S(2)}) copy-start(bf16[64,128,128]{2,1,0:T(8,128)(2,1)} %copy-done) | copy-start | bytes 6291460 | tf_op jit(solution)/shard_map/while
  352.4 0.7 copy-start.5
  352.4 242.1 %copy-start.6 = (s32[512]{0:T(512)S(1)}, s32[512]{0:T(512)}, u32[]{:S(2)}) copy-start(s32[512]{0:T(512)} %param.18) | copy-start | bytes 6148
  357.0 247.1 %all-to-all-start.3 = ((s32[128,1,8]{2,1,0:T(1,128)}), s32[128,1,8]{2,1,0:T(1,128)S(1)}, u32[]{:S(2)}, u32[]{:S(2)}) async-start(s32[128,1,8]{2,1,0:T(1,128)} %bitcast.17), calls=%async_computation.4 | async-start | bytes 131072 | tf_op jit(solution)/shard_map/all_to_all | solution.py:137
  604.0 14.3 %all-to-all-start.5 = ((s32[128,1,8]{2,1,0:T(1,128)}), s32[128,1,8]{2,1,0:T(1,128)S(1)}, u32[]{:S(2)}, u32[]{:S(2)}) async-start(s32[128,1,8]{2,1,0:T(1,128)} %bitcast.30), calls=%async_computation.6 | async-start | bytes 131072 | tf_op jit(solution)/shard_map/all_to_all | solution.py:138
  612.6 36.9 %copy-start.3 = (f32[1,1,1024,128]{3,2,1,0:T(8,128)S(1)}, f32[1,1,1024,128]{3,2,1,0:T(8,128)}, u32[]{:S(2)}) copy-start(f32[1,1,1024,128]{3,2,1,0:T(8,128)} %param.12) | copy-start | bytes 1572868
  618.3 30.9 %all-to-all-start.2 = ((bf16[8,1024,128]{2,1,0:T(8,128)(2,1)}), bf16[8,1024,128]{2,1,0:T(8,128)(2,1)S(1)}, u32[]{:S(2)}, u32[]{:S(2)}) async-start(bf16[8,1024,128]{2,1,0:T(8,128)(2,1)} %bitcast.11), calls=%async_computation.3 | async-start | bytes 4194304 | tf_op jit(solution)/shard_map/all_to_all | solution.py:37
  653.6 41.2 %all-to-all-start.6 = ((bf16[128,8,128]{2,1,0:T(8,128)(2,1)}), bf16[128,8,128]{2,1,0:T(8,128)(2,1)S(1)}, u32[]{:S(2)}, u32[]{:S(2)}) async-start(bf16[128,8,128]{2,1,0:T(8,128)(2,1)} %bitcast.65), calls=%async_computation.7 | async-start | bytes 524288 | tf_op jit(solution)/shard_map/all_to_all | solution.py:146
  690.7 30.7 %copy-start.2 = (f32[2048,128]{1,0:T(8,128)}, f32[2048,128]{1,0:T(8,128)S(1)}, u32[]{:S(2)}) copy-start(f32[2048,128]{1,0:T(8,128)S(1)} %fusion.4) | copy-start | bytes 3145732
  694.8 26.5 %all-to-all-start.4 = ((bf16[128,8,128]{2,1,0:T(8,128)(2,1)}), bf16[128,8,128]{2,1,0:T(8,128)(2,1)S(1)}, u32[]{:S(2)}, u32[]{:S(2)}) async-start(bf16[128,8,128]{2,1,0:T(8,128)(2,1)} %bitcast.66), calls=%async_computation.5 | async-start | bytes 524288 | tf_op jit(solution)/shard_map/all_to_all | solution.py:139
Sparse Core Ops, SparseCore 0:
  352.6 316.8 reduce-scatter.1
